TPU v7x, 32 devices: a whole 2x2x4 slice. The times are simulated.
32 devices in a mesh: seq: 4 (over z), tp: 4 (over x, core), dp: 2 (over y).
Axes of the slice: x: 2, y: 2, z: 4, core: 2. Of those that a mesh axis runs over, the one named last changes fastest.
Arguments:
- queries: bfloat16 [2, 512, 4096], P('dp', 'seq', 'tp'), may hold values from -0.5 to 0.5
- keys: bfloat16 [2, 512, 4096], P('dp', 'seq', 'tp'), may hold values from -0.25 to 0.25
- values: bfloat16 [2, 512, 4096], P('dp', 'seq', 'tp'), may hold values from -19 to 19
- out_gain: float32 [4096], P('tp'), may hold values from 0.1 to 1.9
- grad_out: bfloat16 [2, 512, 4096], P('dp', 'seq', 'tp'), may hold values from -12 to 12
Outputs:
- normed: bfloat16 [2, 512, 4096], P('dp', 'seq', 'tp')
- query_gradient: bfloat16 [2, 512, 4096], P('dp', 'seq', 'tp')
- grad_keys: bfloat16 [2, 512, 4096], P('dp', 'seq', 'tp')
- value_gradient: bfloat16 [2, 512, 4096], P('dp', 'seq', 'tp')
- gain_grad: float32 [4096], P('tp')
All inputs are finite; a program needn't handle non-finite values.
Results may differ from a plain program's by a relative error of at most 0.005.
Values sent between devices are 32-bit elements; how exact they have to be, the bound alone decides.
A program may use at most 64 MiB of HBM per device.

v0:
```python
import jax
import jax.numpy as jnp
from jax import lax
from jax.sharding import PartitionSpec as P

HD = 128
HID = 4096


EPSILON = 1e-06
MATMUL_PRECISION = lax.Precision.HIGHEST


def swapped(array, axis, bit):
    return lax.ppermute(array, axis, [(i, i ^ 1 << bit) for i in range(lax.axis_size(axis))])


def to_heads(matrix):
    row_count = matrix.shape[1]
    block_rows = min(512, row_count)
    shaped = matrix.reshape(row_count // block_rows, block_rows, matrix.shape[2] // HD, HD)
    return shaped.transpose(2, 0, 1, 3)


def from_heads(stacked, like_shape):
    return stacked.transpose(1, 2, 0, 3).reshape(like_shape)


def exclusive_down(block_parts):
    running = jnp.cumsum(block_parts, axis=1)
    return jnp.concatenate([jnp.zeros_like(block_parts), running[:, :-1]], axis=1)


def exclusive_up(block_parts):
    running = jnp.cumsum(block_parts[:, ::-1], axis=1)[:, ::-1]
    return jnp.concatenate([running[:, 1:], jnp.zeros_like(block_parts)], axis=1)


def doubling(totals, backward):
    ordinal = lax.axis_index("seq")
    prefix = jnp.zeros_like(totals)
    for degree in range(lax.axis_size("seq").bit_length() - 1):
        partner = swapped(totals, "seq", degree)
        higher = jnp.bitwise_and(jnp.right_shift(ordinal, degree), 1) == 1
        chosen = jnp.logical_not(higher) if backward else higher
        prefix = prefix + jnp.where(chosen, partner, jnp.zeros_like(partner))
        totals = totals + partner
    return prefix


def prefix_states(totals):
    return doubling(totals, False)


def suffix_states(totals):
    return doubling(totals, True)


def local(queries, keys, values, out_gain, grad_out):
    query_blocks = to_heads(queries)
    key_blocks = to_heads(keys)
    value_blocks = to_heads(values)
    block_len = query_blocks.shape[2]
    causal = jnp.arange(block_len)[:, None] >= jnp.arange(block_len)[None, :]
    block_states = jnp.einsum(
        "hnbd,hnbe->hnde", key_blocks, value_blocks, preferred_element_type=jnp.float32
    )
    earlier = prefix_states(jnp.sum(block_states, axis=1))
    preceding_state_sum = exclusive_down(block_states) + earlier[:, None]
    attention_scores = jnp.einsum(
        "hnid,hnjd->hnij", query_blocks, key_blocks, preferred_element_type=jnp.float32
    )
    attention_scores = jnp.where(causal, attention_scores, 0.0).astype(jnp.bfloat16)
    attention_output = jnp.einsum(
        "hnij,hnje->hnie", attention_scores, value_blocks, preferred_element_type=jnp.float32
    )
    attention_output = attention_output + jnp.einsum(
        "hnid,hnde->hnie",
        query_blocks,
        preceding_state_sum,
        precision=MATMUL_PRECISION,
        preferred_element_type=jnp.float32,
    )
    attention_output = from_heads(attention_output, queries.shape)
    gradient = grad_out.astype(jnp.float32)
    squares = jnp.sum(attention_output * attention_output, axis=2)
    crossed = jnp.sum(gradient * out_gain * attention_output, axis=2)
    squares, crossed = lax.psum((squares, crossed), "tp")
    rescale = lax.rsqrt(squares / HID + EPSILON)[..., None]
    crossed = crossed[..., None]
    normed = (attention_output * rescale * out_gain).astype(jnp.bfloat16)
    gain_part = jnp.sum(gradient * attention_output * rescale, axis=(0, 1))
    gain_grad = lax.psum(gain_part, ("seq", "dp"))
    upstream = (
        out_gain * gradient * rescale
        - attention_output * (rescale * rescale * rescale) * crossed / HID
    )
    upstream_blocks = to_heads(upstream.astype(jnp.bfloat16))
    block_grads = jnp.einsum(
        "hnbd,hnbe->hnde", query_blocks, upstream_blocks, preferred_element_type=jnp.float32
    )
    later_sum = suffix_states(jnp.sum(block_grads, axis=1))
    after_sum = exclusive_up(block_grads) + later_sum[:, None]
    combined_gradient = jnp.einsum(
        "hnie,hnje->hnij", upstream_blocks, value_blocks, preferred_element_type=jnp.float32
    )
    combined_gradient = jnp.where(causal, combined_gradient, 0.0).astype(jnp.bfloat16)
    query_gradient = jnp.einsum(
        "hnij,hnjd->hnid", combined_gradient, key_blocks, preferred_element_type=jnp.float32
    )
    query_gradient = query_gradient + jnp.einsum(
        "hnie,hnde->hnid",
        upstream_blocks,
        preceding_state_sum,
        precision=MATMUL_PRECISION,
        preferred_element_type=jnp.float32,
    )
    grad_keys = jnp.einsum(
        "hnij,hnid->hnjd", combined_gradient, query_blocks, preferred_element_type=jnp.float32
    )
    grad_keys = grad_keys + jnp.einsum(
        "hnje,hnde->hnjd",
        value_blocks,
        after_sum,
        precision=MATMUL_PRECISION,
        preferred_element_type=jnp.float32,
    )
    value_gradient = jnp.einsum(
        "hnij,hnie->hnje", attention_scores, upstream_blocks, preferred_element_type=jnp.float32
    )
    value_gradient = value_gradient + jnp.einsum(
        "hnjd,hnde->hnje",
        key_blocks,
        after_sum,
        precision=MATMUL_PRECISION,
        preferred_element_type=jnp.float32,
    )
    return (
        normed,
        from_heads(query_gradient.astype(jnp.bfloat16), queries.shape),
        from_heads(grad_keys.astype(jnp.bfloat16), queries.shape),
        from_heads(value_gradient.astype(jnp.bfloat16), queries.shape),
        gain_grad,
    )


def solution(mesh):
    return jax.shard_map(
        local,
        mesh=mesh,
        in_specs=(
            P("dp", "seq", "tp"),
            P("dp", "seq", "tp"),
            P("dp", "seq", "tp"),
            P("tp"),
            P("dp", "seq", "tp"),
        ),
        out_specs=(
            P("dp", "seq", "tp"),
            P("dp", "seq", "tp"),
            P("dp", "seq", "tp"),
            P("dp", "seq", "tp"),
            P("tp"),
        ),
        check_vma=False,
    )
```

profile of v0, /device:TPU:12, one launch (start us, length us, event | category | flops | bytes accessed | tf_op | source)
XLA Modules:
  0.0 112.3 jit_solution(13165341184376400823)
XLA Ops:
  0.6 1.0 copy.52
  1.7 0.9 copy-done.1
  3.5 13.1 %collective-permute-done = f32[8,128,128]{2,1,0:T(8,128)S(1)} collective-permute-done((f32[8,128,128]{2,1,0:T(8,128)S(1)}, f32[8,128,128]{2,1,0:T(8,128)S(1)}, u32[]{:S(2)}, u32[]{:S(2)}) %collective-permute-start) | collective-permute-done | bytes 524320 | tf_op jit(solution)/shard_map/ppermute | solution.py:15
  16.6 0.8 add.42
  17.4 2.6 %collective-permute-start.1 = (f32[8,128,128]{2,1,0:T(8,128)}, f32[8,128,128]{2,1,0:T(8,128)S(1)}, u32[]{:S(2)}, u32[]{:S(2)}) collective-permute-start(f32[8,128,128]{2,1,0:T(8,128)} %add.42), channel_id=1, source_target_pairs={{0,16},{8,24},{16,0},{24,8},{1,17},{9,25},{17,1},{25,9},{2,18},{10... | collective-permute-start | bytes 1572872 | tf_op jit(solution)/shard_map/ppermute | solution.py:15
  20.1 0.9 copy-done.6
  22.0 19.8 %collective-permute-done.1 = f32[8,128,128]{2,1,0:T(8,128)S(1)} collective-permute-done((f32[8,128,128]{2,1,0:T(8,128)}, f32[8,128,128]{2,1,0:T(8,128)S(1)}, u32[]{:S(2)}, u32[]{:S(2)}) %collective-permute-start.1) | collective-permute-done | bytes 524320 | tf_op jit(solution)/shard_map/ppermute | solution.py:15
  41.8 0.6 fusion.15
  42.4 6.9 %psum.23 = f32[1,128]{1,0:T(1,128)S(1)} all-reduce(f32[1,128]{1,0:T(1,128)S(1)} %bitcast.163), channel_id=1, replica_groups=mesh['seq'=4,'tp'=4,'dp'=2] {'tp'}, use_global_device_ids=true, to_apply=%region_1.2 | all-reduce | flops 128 | bytes 1024 | tf_op jit(solution)/shard_map/psum | solution.py:88
  49.5 0.7 copy-done.2
  50.5 5.9 %psum.25 = f32[128]{0:T(128)S(1)} all-reduce(f32[128]{0:T(128)S(1)} %get-tuple-element.11), channel_id=1, replica_groups=mesh['seq'=4,'tp'=4,'dp'=2] {'tp'}, use_global_device_ids=true, to_apply=%region_3.4 | all-reduce | flops 128 | bytes 1024 | tf_op jit(solution)/shard_map/psum | solution.py:88
  56.4 0.9 fusion.11
  57.8 0.8 collective-permute-start.2
  58.6 0.7 bitcast_bitcast_fusion
  60.0 11.3 %collective-permute-done.2 = f32[8,128,128]{2,1,0:T(8,128)S(1)} collective-permute-done((f32[8,128,128]{2,1,0:T(8,128)S(1)}, f32[8,128,128]{2,1,0:T(8,128)S(1)}, u32[]{:S(2)}, u32[]{:S(2)}) %collective-permute-start.2) | collective-permute-done | bytes 524320 | tf_op jit(solution)/shard_map/ppermute | solution.py:15
  71.3 0.8 add.49
  72.2 3.3 %collective-permute-start.3 = (f32[8,128,128]{2,1,0:T(8,128)}, f32[8,128,128]{2,1,0:T(8,128)S(1)}, u32[]{:S(2)}, u32[]{:S(2)}) collective-permute-start(f32[8,128,128]{2,1,0:T(8,128)} %add.49), channel_id=1, source_target_pairs={{0,16},{8,24},{16,0},{24,8},{1,17},{9,25},{17,1},{25,9},{2,18},{10... | collective-permute-start | bytes 1572872 | tf_op jit(solution)/shard_map/ppermute | solution.py:15
  75.9 0.9 copy.27
  76.7 31.2 %psum.26 = f32[1024]{0:T(1024)} all-reduce(f32[1024]{0:T(1024)S(1)} %get-tuple-element.10), channel_id=1, replica_groups=mesh['seq'=4,'tp'=4,'dp'=2] {'seq','dp'}, use_global_device_ids=true, to_apply=%region_5.6 | all-reduce | flops 1024 | bytes 8192 | tf_op jit(solution)/shard_map/psum | solution.py:93
  108.2 0.7 copy-done.3
  109.2 0.7 fusion.5
  109.9 0.9 copy.28
  110.8 0.6 fusion.4
  111.4 0.9 copy.29
  (35 shorter events, 4.5 us)
Async XLA Ops:
  1.6 1.0 copy-start.1
  2.9 13.7 %collective-permute-start = (f32[8,128,128]{2,1,0:T(8,128)S(1)}, f32[8,128,128]{2,1,0:T(8,128)S(1)}, u32[]{:S(2)}, u32[]{:S(2)}) collective-permute-start(f32[8,128,128]{2,1,0:T(8,128)S(1)} %fusion.16), channel_id=1, source_target_pairs={{0,8},{8,0},{16,24},{24,16},{1,9},{9,1},{17,25},{25,17},{2,10},{10... | collective-permute-start | bytes 1572872 | tf_op jit(solution)/shard_map/ppermute | solution.py:15
  3.5 16.6 %copy-start = (bf16[1,128,1024]{2,1,0:T(8,128)(2,1)S(1)}, bf16[1,128,1024]{2,1,0:T(8,128)(2,1)}, u32[]{:S(2)}) copy-start(bf16[1,128,1024]{2,1,0:T(8,128)(2,1)} %param.5) | copy-start | bytes 786436
  17.4 24.4 %collective-permute-start.1 = (f32[8,128,128]{2,1,0:T(8,128)}, f32[8,128,128]{2,1,0:T(8,128)S(1)}, u32[]{:S(2)}, u32[]{:S(2)}) collective-permute-start(f32[8,128,128]{2,1,0:T(8,128)} %add.42), channel_id=1, source_target_pairs={{0,16},{8,24},{16,0},{24,8},{1,17},{9,25},{17,1},{25,9},{2,18},{10... | collective-permute-start | bytes 1572872 | tf_op jit(solution)/shard_map/ppermute | solution.py:15
  20.1 1.0 copy-start.6
  21.3 0.7 copy-start.4
  49.3 1.0 copy-start.2
  49.3 1.0 copy-start.8
  57.8 13.5 %collective-permute-start.2 = (f32[8,128,128]{2,1,0:T(8,128)S(1)}, f32[8,128,128]{2,1,0:T(8,128)S(1)}, u32[]{:S(2)}, u32[]{:S(2)}) collective-permute-start(f32[8,128,128]{2,1,0:T(8,128)S(1)} %convolution_bitcast_fusion.2), channel_id=1, source_target_pairs={{0,8},{8,0},{16,24},{24,16},{1,9},{9,1},{17,25},{25,17},{2,10},{10... | collective-permute-start | bytes 1572872 | tf_op jit(solution)/shard_map/ppermute | solution.py:15
  72.2 37.0 %collective-permute-start.3 = (f32[8,128,128]{2,1,0:T(8,128)}, f32[8,128,128]{2,1,0:T(8,128)S(1)}, u32[]{:S(2)}, u32[]{:S(2)}) collective-permute-start(f32[8,128,128]{2,1,0:T(8,128)} %add.49), channel_id=1, source_target_pairs={{0,16},{8,24},{16,0},{24,8},{1,17},{9,25},{17,1},{25,9},{2,18},{10... | collective-permute-start | bytes 1572872 | tf_op jit(solution)/shard_map/ppermute | solution.py:15
  75.9 32.1 %copy-start.5 = (bf16[8,128,128]{2,1,0:T(8,128)(2,1)S(1)}, bf16[8,128,128]{2,1,0:T(8,128)(2,1)}, u32[]{:S(2)}) copy-start(bf16[8,128,128]{2,1,0:T(8,128)(2,1)} %copy-done.4) | copy-start | bytes 786436
  108.0 1.0 copy-start.3
  109.9 1.0 copy-start.7
where the time goes:
time: 113 us; the launch traced here: 112 us
  waiting for transfers between devices  44.2 us (39%)
  blocking collectives  44 us (39%)
  local copies, waits for them, and re-layouts  8.52 us (8%)
  starting transfers between devices  7.21 us (6%)
  matrix products  4.67 us (4%)
  other arithmetic  2.87 us (3%)
    ppermute x4, waiting for transfers between devices, swapped(): lax.ppermute(array, axis, [(i, i ^ 1 << bit) for i in range(lax.axis_size...  44.2 us
    psum x1, blocking collectives, local(): gain_grad = lax.psum(gain_part, ('seq', 'dp'))  31.2 us
    psum x2, blocking collectives, local(): squares, crossed = lax.psum((squares, crossed), 'tp')  12.8 us
    unnamed x24, local copies, waits for them, and re-layouts  7.4 us
    ppermute x4, starting transfers between devices, swapped(): lax.ppermute(array, axis, [(i, i ^ 1 << bit) for i in range(lax.axis_size...  7.21 us
  transfers between devices with their start and end apart: 4, of which 3 were waited for; matrix products, arithmetic and copies ran while one was open for 3% of the time, Pallas kernels for 0%

commit v1 on v0

v1 whole, which is shorter than its diff:
```python
import functools

import jax
import jax.numpy as jnp
from jax import lax
from jax.experimental import pallas as pl
from jax.experimental.pallas import tpu as pltpu
from jax.sharding import PartitionSpec as P

HD = 128
HID = 4096
EPSILON = 1e-06
MESH = pl.DeviceIdType.MESH
F32 = jnp.float32
BF16 = jnp.bfloat16


def dot(a, b, ca, cb):
    return lax.dot_general(a, b, (((ca,), (cb,)), ((), ())), preferred_element_type=F32)


def split(x):
    high = x.astype(BF16)
    return high, (x - high.astype(F32)).astype(BF16)


def dot_wide(a, x, ca, cb):
    high, low = split(x)
    return dot(a, high, ca, cb) + dot(a, low, ca, cb)


def kernel(
    n_seq, n_tp, n_dp,
    q_in, k_in, v_in, gain_in, g_in,
    normed_out, dq_out, dk_out, dv_out, gg_out,
    q_ref, k_ref, v_ref, gain_ref, g_ref,
    prior, total, later, total_back,
    att, scores, up, normed, dq, dk, dv,
    stat, gain_seq, gain_dp, gg,
    in_sem, out_sem,
    up_send, up_recv, down_send, down_recv,
    stat_send, stat_recv, gs_send, gs_recv, gd_send, gd_recv,
):
    rows, width = q_ref.shape
    heads = width // HD
    z = lax.axis_index("seq")
    t = lax.axis_index("tp")
    d = lax.axis_index("dp")
    first, last = z == 0, z == n_seq - 1
    above = lax.rem(z + 1, n_seq)
    below = lax.rem(z + n_seq - 1, n_seq)

    def head(h):
        return slice(h * HD, (h + 1) * HD)

    def peers(axis, me, size):
        return [{axis: lax.rem(me + i, size)} for i in range(1, size)]

    everyone = peers("seq", z, n_seq) + peers("tp", t, n_tp) + peers("dp", d, n_dp)
    barrier = pltpu.get_barrier_semaphore()
    for peer in everyone:
        pl.semaphore_signal(barrier, inc=1, device_id=peer, device_id_type=MESH)

    loads = [
        pltpu.make_async_copy(src, dst, in_sem.at[i])
        for i, (src, dst) in enumerate(
            [(k_in, k_ref), (v_in, v_ref), (q_in, q_ref), (g_in, g_ref), (gain_in, gain_ref)]
        )
    ]
    for load in loads:
        load.start()
    loads[0].wait()
    loads[1].wait()

    def move_up(h):
        return pltpu.make_async_remote_copy(
            src_ref=total.at[h], dst_ref=prior.at[h],
            send_sem=up_send.at[h], recv_sem=up_recv.at[h],
            device_id={"seq": above}, device_id_type=MESH,
        )

    def move_down(h):
        return pltpu.make_async_remote_copy(
            src_ref=total_back.at[h], dst_ref=later.at[h],
            send_sem=down_send.at[h], recv_sem=down_recv.at[h],
            device_id={"seq": below}, device_id_type=MESH,
        )

    for h in range(heads):
        total[h] = dot(k_ref[:, head(h)], v_ref[:, head(h)], 0, 0)
        if h == 0:
            pl.semaphore_wait(barrier, len(everyone))
        if n_seq > 1:
            @pl.when(first)
            def _():
                move_up(h).start()

    @pl.when(first)
    def _():
        prior[...] = jnp.zeros_like(prior)

    @pl.when(last)
    def _():
        later[...] = jnp.zeros_like(later)

    loads[2].wait()
    loads[3].wait()
    loads[4].wait()
    causal = lax.broadcasted_iota(jnp.int32, (rows, rows), 0) >= lax.broadcasted_iota(
        jnp.int32, (rows, rows), 1
    )
    squares = jnp.zeros((rows, HD), F32)
    crossed = jnp.zeros((rows, HD), F32)
    for h in range(heads):
        if n_seq > 1:
            @pl.when(jnp.logical_not(first))
            def _():
                move_up(h).wait_recv()

                @pl.when(jnp.logical_not(last))
                def _():
                    total[h] = total[h] + prior[h]
                    move_up(h).start()

        q = q_ref[:, head(h)]
        v = v_ref[:, head(h)]
        score = jnp.where(causal, dot(q, k_ref[:, head(h)], 1, 1), 0.0).astype(BF16)
        scores[h] = score
        out = dot(score, v, 1, 0) + dot_wide(q, prior[h], 1, 0)
        att[:, head(h)] = out
        squares = squares + out * out
        crossed = crossed + g_ref[:, head(h)].astype(F32) * gain_ref[h:h + 1, :] * out

    stat[t, 0:1, :] = jnp.sum(squares.T, axis=0, keepdims=True)
    stat[t, 1:2, :] = jnp.sum(crossed.T, axis=0, keepdims=True)

    def all_send(buffer, axis, me, size, send, recv):
        return [
            pltpu.make_async_remote_copy(
                src_ref=buffer.at[me], dst_ref=buffer.at[me],
                send_sem=send.at[i - 1], recv_sem=recv.at[i - 1],
                device_id={axis: lax.rem(me + i, size)}, device_id_type=MESH,
            )
            for i in range(1, size)
        ]

    stat_moves = all_send(stat, "tp", t, n_tp, stat_send, stat_recv)
    for move in stat_moves:
        move.start()
    for move in stat_moves:
        move.wait_recv()
    sums = stat[0, 0:2, :]
    for i in range(1, n_tp):
        sums = sums + stat[i, 0:2, :]
    scale_row = lax.rsqrt(sums[0:1] / HID + EPSILON)
    factor_row = scale_row * scale_row * scale_row * sums[1:2] / HID
    scale = jnp.broadcast_to(scale_row, (HD, rows)).T
    factor = jnp.broadcast_to(factor_row, (HD, rows)).T

    def upstream(h):
        out = att[:, head(h)]
        grad = g_ref[:, head(h)].astype(F32)
        scaled = grad * scale
        up[:, head(h)] = (gain_ref[h:h + 1, :] * scaled - out * factor).astype(BF16)
        gain_seq[z, h:h + 1, :] = jnp.sum(scaled * out, axis=0, keepdims=True)

    def back_state(h):
        total_back[h] = dot(q_ref[:, head(h)], up[:, head(h)], 0, 0)
        if n_seq > 1:
            @pl.when(last)
            def _():
                move_down(h).start()

    upstream(0)
    back_state(0)
    for h in range(1, heads):
        upstream(h)
    seq_moves = all_send(gain_seq, "seq", z, n_seq, gs_send, gs_recv)
    for move in seq_moves:
        move.start()
    for h in range(1, heads):
        back_state(h)

    dp_moves = all_send(gain_dp, "dp", d, n_dp, gd_send, gd_recv)
    stores = []

    def store(src, dst):
        copy = pltpu.make_async_copy(src, dst, out_sem.at[len(stores)])
        copy.start()
        stores.append(copy)

    for h in range(heads):
        if n_seq > 1:
            @pl.when(jnp.logical_not(last))
            def _():
                move_down(h).wait_recv()

                @pl.when(jnp.logical_not(first))
                def _():
                    total_back[h] = total_back[h] + later[h]
                    move_down(h).start()

        q, k, v, u = (ref[:, head(h)] for ref in (q_ref, k_ref, v_ref, up))
        normed[:, head(h)] = (att[:, head(h)] * scale * gain_ref[h:h + 1, :]).astype(BF16)
        mixed = jnp.where(causal, dot(u, v, 1, 1), 0.0).astype(BF16)
        dq[:, head(h)] = (dot(mixed, k, 1, 0) + dot_wide(u, prior[h], 1, 1)).astype(BF16)
        high, low = split(later[h])
        dk[:, head(h)] = (
            dot(mixed, q, 0, 0) + dot(v, high, 1, 1) + dot(v, low, 1, 1)
        ).astype(BF16)
        dv[:, head(h)] = (
            dot(scores[h], u, 0, 0) + dot(k, high, 1, 0) + dot(k, low, 1, 0)
        ).astype(BF16)
        for src, dst in ((normed, normed_out), (dq, dq_out), (dk, dk_out), (dv, dv_out)):
            store(src.at[:, head(h)], dst.at[:, head(h)])
        if h == heads // 2:
            for move in seq_moves:
                move.wait_recv()
            gain_sum = gain_seq[0]
            for i in range(1, n_seq):
                gain_sum = gain_sum + gain_seq[i]
            gain_dp[d] = gain_sum
            for move in dp_moves:
                move.start()

    for move in dp_moves:
        move.wait_recv()
    gain_sum = gain_dp[0]
    for i in range(1, n_dp):
        gain_sum = gain_sum + gain_dp[i]
    gg[...] = gain_sum
    store(gg, gg_out)

    for move in stat_moves + seq_moves + dp_moves:
        move.wait_send()
    if n_seq > 1:
        @pl.when(jnp.logical_not(last))
        def _():
            for h in range(heads):
                move_up(h).wait_send()

        @pl.when(jnp.logical_not(first))
        def _():
            for h in range(heads):
                move_down(h).wait_send()
    for copy in stores:
        copy.wait()


def solution(mesh):
    n_seq, n_tp, n_dp = (mesh.shape[name] for name in ("seq", "tp", "dp"))

    def local(queries, keys, values, out_gain, grad_out):
        shape = queries.shape
        rows, width = shape[0] * shape[1], shape[2]
        heads = width // HD
        matrix = jax.ShapeDtypeStruct((rows, width), BF16)
        state = pltpu.VMEM((heads, HD, HD), F32)
        page = pltpu.VMEM((rows, width), BF16)
        sems = pltpu.SemaphoreType.DMA
        flat = lambda x: x.reshape(rows, width)
        outs = pl.pallas_call(
            functools.partial(kernel, n_seq, n_tp, n_dp),
            out_shape=(matrix,) * 4 + (jax.ShapeDtypeStruct((heads, HD), F32),),
            in_specs=[pl.BlockSpec(memory_space=pl.ANY)] * 5,
            out_specs=[pl.BlockSpec(memory_space=pl.ANY)] * 5,
            scratch_shapes=[
                page, page, page, pltpu.VMEM((heads, HD), F32), page,
                state, state, state, state,
                pltpu.VMEM((rows, width), F32),
                pltpu.VMEM((heads, rows, rows), BF16),
                page, page, page, page, page,
                pltpu.VMEM((n_tp, 8, rows), F32),
                pltpu.VMEM((n_seq, heads, HD), F32),
                pltpu.VMEM((n_dp, heads, HD), F32),
                pltpu.VMEM((heads, HD), F32),
                sems((5,)), sems((4 * heads + 1,)),
                sems((heads,)), sems((heads,)), sems((heads,)), sems((heads,)),
                sems((max(n_tp - 1, 1),)), sems((max(n_tp - 1, 1),)),
                sems((max(n_seq - 1, 1),)), sems((max(n_seq - 1, 1),)),
                sems((max(n_dp - 1, 1),)), sems((max(n_dp - 1, 1),)),
            ],
            compiler_params=pltpu.CompilerParams(collective_id=0, has_side_effects=True),
        )(flat(queries), flat(keys), flat(values), out_gain.reshape(heads, HD), flat(grad_out))
        return tuple(x.reshape(shape) for x in outs[:4]) + (outs[4].reshape(width),)

    spec = P("dp", "seq", "tp")
    return jax.shard_map(
        local,
        mesh=mesh,
        in_specs=(spec, spec, spec, P("tp"), spec),
        out_specs=(spec, spec, spec, spec, P("tp")),
        check_vma=False,
    )
```

time: 113 us -> 56.8 us (0.50)
  the two profiles are of different devices: /device:TPU:12 before, /device:TPU:0 now
where the time goes in v1:
time: 56.8 us; the launch traced here: 56.6 us
  Pallas kernels  50.8 us (89%)
  local copies, waits for them, and re-layouts  5.1 us (9%)
  between operations  0.65 us (1%)
    pallas_call x1, Pallas kernels, local(): pl.pallas_call(functools.partial(kernel, n_seq, n_tp, n_dp), out_shape=(m...  50.8 us
    unnamed x13, local copies, waits for them, and re-layouts  5.1 us

profile of v1, /device:TPU:0, one launch (start us, length us, event | category | flops | bytes accessed | tf_op | source)
XLA Modules:
  0.0 56.6 jit_solution(2963439634158948922)
XLA Ops:
  0.6 50.8 %shard_map.92 = (bf16[128,1024]{1,0:T(8,128)(2,1)}, bf16[128,1024]{1,0:T(8,128)(2,1)}, bf16[128,1024]{1,0:T(8,128)(2,1)}, bf16[128,1024]{1,0:T(8,128)(2,1)}, f32[8,128]{1,0:T(8,128)}) custom-call(bf16[128,1024]{1,0:T(8,128)(2,1)} %bitcast.14, bf16[128,1024]{1,0:T(8,128)(2,1)} %bitcast.15, bf16[128,1024]{1,0:T(8,128)(2,1)} %bitcast.16, f32[8,128]{1,0:T(8,128)} %bitcast.18, ...), custom_call_target="tpu_custom_call" | custom-call | tf_op jit(solution)/shard_map/pallas_call | solution.py:262
  51.5 0.0 copy-start.2
  51.5 1.7 %copy.15 = bf16[1,128,1024]{2,1,0:T(8,128)(2,1)} copy(bf16[1,128,1024]{2,1,0:T(8,128)(2,1)} %bitcast.13) | data formatting | bytes 524288
  53.2 0.0 copy-done.2
  53.2 0.0 copy-start.1
  53.2 0.7 %copy.16 = bf16[1,128,1024]{2,1,0:T(8,128)(2,1)} copy(bf16[1,128,1024]{2,1,0:T(8,128)(2,1)S(1)} %bitcast.12) | data formatting | bytes 524288
  53.9 0.3 copy-done.1
  54.2 0.0 copy-start
  54.2 0.7 %copy.17 = bf16[1,128,1024]{2,1,0:T(8,128)(2,1)} copy(bf16[1,128,1024]{2,1,0:T(8,128)(2,1)S(1)} %bitcast.11) | data formatting | bytes 524288
  54.9 0.3 copy-done
  55.3 0.0 copy-start.3
  55.3 0.7 %copy.18 = bf16[1,128,1024]{2,1,0:T(8,128)(2,1)} copy(bf16[1,128,1024]{2,1,0:T(8,128)(2,1)S(1)} %bitcast.10) | data formatting | bytes 524288
  56.0 0.0 copy-done.3
  56.0 0.6 %copy.19 = f32[1024]{0:T(1024)} copy(f32[1024]{0:T(1024)S(1)} %bitcast.19) | data formatting | bytes 8192
Async XLA Ops:
  51.5 1.7 %copy-start.2 = (bf16[128,1024]{1,0:T(8,128)(2,1)S(1)}, bf16[128,1024]{1,0:T(8,128)(2,1)}, u32[]{:S(2)}) copy-start(bf16[128,1024]{1,0:T(8,128)(2,1)} %get-tuple-element.11) | copy-start | bytes 786436
  53.2 1.0 %copy-start.1 = (bf16[128,1024]{1,0:T(8,128)(2,1)S(1)}, bf16[128,1024]{1,0:T(8,128)(2,1)}, u32[]{:S(2)}) copy-start(bf16[128,1024]{1,0:T(8,128)(2,1)} %get-tuple-element.12) | copy-start | bytes 786436
  54.2 1.0 %copy-start = (bf16[128,1024]{1,0:T(8,128)(2,1)S(1)}, bf16[128,1024]{1,0:T(8,128)(2,1)}, u32[]{:S(2)}) copy-start(bf16[128,1024]{1,0:T(8,128)(2,1)} %get-tuple-element.13) | copy-start | bytes 786436
  55.3 0.7 %copy-start.3 = (f32[8,128]{1,0:T(8,128)S(1)}, f32[8,128]{1,0:T(8,128)}, u32[]{:S(2)}) copy-start(f32[8,128]{1,0:T(8,128)} %get-tuple-element.14) | copy-start | bytes 12292

commit v2 on v1

--- a/solution.py
+++ b/solution.py
@@ -10,6 +10,8 @@
 HD = 128
 HID = 4096
 EPSILON = 1e-06
+PIECES = 4
+PART = HD // PIECES
 MESH = pl.DeviceIdType.MESH
 F32 = jnp.float32
 BF16 = jnp.bfloat16
@@ -35,7 +37,7 @@
     normed_out, dq_out, dk_out, dv_out, gg_out,
     q_ref, k_ref, v_ref, gain_ref, g_ref,
     prior, total, later, total_back,
-    att, scores, up, normed, dq, dk, dv,
+    att, scores, mixed, squares, crossed, dk_part, dv_part, up, normed, dq, dk, dv,
     stat, gain_seq, gain_dp, gg,
     in_sem, out_sem,
     up_send, up_recv, down_send, down_recv,
@@ -72,19 +74,42 @@
     loads[0].wait()
     loads[1].wait()
 
-    def move_up(h):
+    def part(p):
+        return slice(p * PART, (p + 1) * PART)
+
+    def move_up(h, p):
+        i = h * PIECES + p
         return pltpu.make_async_remote_copy(
-            src_ref=total.at[h], dst_ref=prior.at[h],
-            send_sem=up_send.at[h], recv_sem=up_recv.at[h],
+            src_ref=total.at[h, part(p)], dst_ref=prior.at[h, part(p)],
+            send_sem=up_send.at[i], recv_sem=up_recv.at[i],
             device_id={"seq": above}, device_id_type=MESH,
         )
 
-    def move_down(h):
+    def move_down(h, p):
+        i = h * PIECES + p
         return pltpu.make_async_remote_copy(
-            src_ref=total_back.at[h], dst_ref=later.at[h],
-            send_sem=down_send.at[h], recv_sem=down_recv.at[h],
+            src_ref=total_back.at[h, part(p)], dst_ref=later.at[h, part(p)],
+            send_sem=down_send.at[i], recv_sem=down_recv.at[i],
             device_id={"seq": below}, device_id_type=MESH,
         )
+
+    def relay(h, p, mine, come, move, is_first, is_last):
+        @pl.when(jnp.logical_and(jnp.logical_not(is_first), jnp.logical_not(is_last)))
+        def _():
+            move(h, p).wait_recv()
+            mine[h, part(p)] = mine[h, part(p)] + come[h, part(p)]
+            move(h, p).start()
+
+        @pl.when(jnp.logical_and(is_last, jnp.logical_not(is_first)))
+        def _():
+            move(h, p).wait_recv()
+
+    def relay_all(mine, come, move, is_first, is_last, slots):
+        for h in range(heads):
+            for p in range(PIECES):
+                relay(h, p, mine, come, move, is_first, is_last)
+                for step in slots[h * PIECES + p]:
+                    step()
 
     for h in range(heads):
         total[h] = dot(k_ref[:, head(h)], v_ref[:, head(h)], 0, 0)
@@ -93,7 +118,8 @@
         if n_seq > 1:
             @pl.when(first)
             def _():
-                move_up(h).start()
+                for p in range(PIECES):
+                    move_up(h, p).start()
 
     @pl.when(first)
     def _():
@@ -109,30 +135,36 @@
     causal = lax.broadcasted_iota(jnp.int32, (rows, rows), 0) >= lax.broadcasted_iota(
         jnp.int32, (rows, rows), 1
     )
-    squares = jnp.zeros((rows, HD), F32)
-    crossed = jnp.zeros((rows, HD), F32)
+    def score_of(h):
+        score = jnp.where(causal, dot(q_ref[:, head(h)], k_ref[:, head(h)], 1, 1), 0.0)
+        scores[h] = score.astype(BF16)
+
+    def attend_block(h):
+        att[:, head(h)] = dot(scores[h], v_ref[:, head(h)], 1, 0)
+
+    def attend_prior(h):
+        att[:, head(h)] = att[:, head(h)] + dot_wide(q_ref[:, head(h)], prior[h], 1, 0)
+
+    def add_stats(h):
+        out = att[:, head(h)]
+        square = out * out
+        cross = g_ref[:, head(h)].astype(F32) * gain_ref[h:h + 1, :] * out
+        squares[...] = square if h == 0 else squares[...] + square
+        crossed[...] = cross if h == 0 else crossed[...] + cross
+
+    slots = [[] for _ in range(heads * PIECES)]
     for h in range(heads):
-        if n_seq > 1:
-            @pl.when(jnp.logical_not(first))
-            def _():
-                move_up(h).wait_recv()
-
-                @pl.when(jnp.logical_not(last))
-                def _():
-                    total[h] = total[h] + prior[h]
-                    move_up(h).start()
-
-        q = q_ref[:, head(h)]
-        v = v_ref[:, head(h)]
-        score = jnp.where(causal, dot(q, k_ref[:, head(h)], 1, 1), 0.0).astype(BF16)
-        scores[h] = score
-        out = dot(score, v, 1, 0) + dot_wide(q, prior[h], 1, 0)
-        att[:, head(h)] = out
-        squares = squares + out * out
-        crossed = crossed + g_ref[:, head(h)].astype(F32) * gain_ref[h:h + 1, :] * out
-
-    stat[t, 0:1, :] = jnp.sum(squares.T, axis=0, keepdims=True)
-    stat[t, 1:2, :] = jnp.sum(crossed.T, axis=0, keepdims=True)
+        slots[h * PIECES].append(functools.partial(score_of, h))
+        slots[h * PIECES + 1].append(functools.partial(attend_block, h))
+        if h > 0:
+            slots[h * PIECES + 2].append(functools.partial(attend_prior, h - 1))
+            slots[h * PIECES + 3].append(functools.partial(add_stats, h - 1))
+    relay_all(total, prior, move_up, first, last, slots)
+    attend_prior(heads - 1)
+    add_stats(heads - 1)
+
+    stat[t, 0:1, :] = jnp.sum(squares[...].T, axis=0, keepdims=True)
+    stat[t, 1:2, :] = jnp.sum(crossed[...].T, axis=0, keepdims=True)
 
     def all_send(buffer, axis, me, size, send, recv):
         return [
@@ -169,7 +201,8 @@
         if n_seq > 1:
             @pl.when(last)
             def _():
-                move_down(h).start()
+                for p in range(PIECES):
+                    move_down(h, p).start()
 
     upstream(0)
     back_state(0)
@@ -189,39 +222,63 @@
         copy.start()
         stores.append(copy)
 
+    def normed_of(h):
+        normed[:, head(h)] = (att[:, head(h)] * scale * gain_ref[h:h + 1, :]).astype(BF16)
+        store(normed.at[:, head(h)], normed_out.at[:, head(h)])
+
+    def mixed_of(h):
+        mix = jnp.where(causal, dot(up[:, head(h)], v_ref[:, head(h)], 1, 1), 0.0)
+        mixed[h] = mix.astype(BF16)
+
+    def dq_of(h):
+        dq[:, head(h)] = (
+            dot(mixed[h], k_ref[:, head(h)], 1, 0) + dot_wide(up[:, head(h)], prior[h], 1, 1)
+        ).astype(BF16)
+        store(dq.at[:, head(h)], dq_out.at[:, head(h)])
+
+    def block_parts(h):
+        dk_part[h] = dot(mixed[h], q_ref[:, head(h)], 0, 0)
+        dv_part[h] = dot(scores[h], up[:, head(h)], 0, 0)
+
+    def dk_of(h):
+        wide = dot_wide(v_ref[:, head(h)], later[h], 1, 1)
+        dk[:, head(h)] = (dk_part[h] + wide).astype(BF16)
+        store(dk.at[:, head(h)], dk_out.at[:, head(h)])
+
+    def dv_of(h):
+        wide = dot_wide(k_ref[:, head(h)], later[h], 1, 0)
+        dv[:, head(h)] = (dv_part[h] + wide).astype(BF16)
+        store(dv.at[:, head(h)], dv_out.at[:, head(h)])
+
+    def gain_middle():
+        for move in seq_moves:
+            move.wait_recv()
+        gain_sum = gain_seq[0]
+        for i in range(1, n_seq):
+            gain_sum = gain_sum + gain_seq[i]
+        gain_dp[d] = gain_sum
+        for move in dp_moves:
+            move.start()
+
+    block_work = [
+        functools.partial(work, h)
+        for h in range(heads)
+        for work in (mixed_of, dq_of, block_parts, normed_of)
+    ]
+    half = 2 * heads
+    for step in block_work[:half]:
+        step()
+    slots = [[] for _ in range(heads * PIECES)]
     for h in range(heads):
-        if n_seq > 1:
-            @pl.when(jnp.logical_not(last))
-            def _():
-                move_down(h).wait_recv()
-
-                @pl.when(jnp.logical_not(first))
-                def _():
-                    total_back[h] = total_back[h] + later[h]
-                    move_down(h).start()
-
-        q, k, v, u = (ref[:, head(h)] for ref in (q_ref, k_ref, v_ref, up))
-        normed[:, head(h)] = (att[:, head(h)] * scale * gain_ref[h:h + 1, :]).astype(BF16)
-        mixed = jnp.where(causal, dot(u, v, 1, 1), 0.0).astype(BF16)
-        dq[:, head(h)] = (dot(mixed, k, 1, 0) + dot_wide(u, prior[h], 1, 1)).astype(BF16)
-        high, low = split(later[h])
-        dk[:, head(h)] = (
-            dot(mixed, q, 0, 0) + dot(v, high, 1, 1) + dot(v, low, 1, 1)
-        ).astype(BF16)
-        dv[:, head(h)] = (
-            dot(scores[h], u, 0, 0) + dot(k, high, 1, 0) + dot(k, low, 1, 0)
-        ).astype(BF16)
-        for src, dst in ((normed, normed_out), (dq, dq_out), (dk, dk_out), (dv, dv_out)):
-            store(src.at[:, head(h)], dst.at[:, head(h)])
-        if h == heads // 2:
-            for move in seq_moves:
-                move.wait_recv()
-            gain_sum = gain_seq[0]
-            for i in range(1, n_seq):
-                gain_sum = gain_sum + gain_seq[i]
-            gain_dp[d] = gain_sum
-            for move in dp_moves:
-                move.start()
+        if h > 0:
+            slots[h * PIECES].append(functools.partial(dk_of, h - 1))
+            slots[h * PIECES + 1].append(functools.partial(dv_of, h - 1))
+        slots[h * PIECES + 2].append(block_work[half + 2 * h])
+        slots[h * PIECES + 3].append(block_work[half + 2 * h + 1])
+    slots[(3 * heads // 4) * PIECES].append(gain_middle)
+    relay_all(total_back, later, move_down, last, first, slots)
+    dk_of(heads - 1)
+    dv_of(heads - 1)
 
     for move in dp_moves:
         move.wait_recv()
@@ -237,13 +294,23 @@
         @pl.when(jnp.logical_not(last))
         def _():
             for h in range(heads):
-                move_up(h).wait_send()
+                for p in range(PIECES):
+                    move_up(h, p).wait_send()
 
         @pl.when(jnp.logical_not(first))
         def _():
             for h in range(heads):
-                move_down(h).wait_send()
+                for p in range(PIECES):
+                    move_down(h, p).wait_send()
     for copy in stores:
+        copy.wait()
+
+
+def write_out(*refs):
+    copies = [pltpu.make_async_copy(refs[i], refs[5 + i], refs[10].at[i]) for i in range(5)]
+    for copy in copies:
+        copy.start()
+    for copy in copies:
         copy.wait()
 
 
@@ -254,6 +321,7 @@
         shape = queries.shape
         rows, width = shape[0] * shape[1], shape[2]
         heads = width // HD
+        chunks = heads * PIECES
         matrix = jax.ShapeDtypeStruct((rows, width), BF16)
         state = pltpu.VMEM((heads, HD, HD), F32)
         page = pltpu.VMEM((rows, width), BF16)
@@ -262,26 +330,45 @@
         outs = pl.pallas_call(
             functools.partial(kernel, n_seq, n_tp, n_dp),
             out_shape=(matrix,) * 4 + (jax.ShapeDtypeStruct((heads, HD), F32),),
-            in_specs=[pl.BlockSpec(memory_space=pl.ANY)] * 5,
+            in_specs=[pl.BlockSpec(memory_space=pltpu.HBM)] * 5,
             out_specs=[pl.BlockSpec(memory_space=pl.ANY)] * 5,
             scratch_shapes=[
                 page, page, page, pltpu.VMEM((heads, HD), F32), page,
                 state, state, state, state,
                 pltpu.VMEM((rows, width), F32),
-                pltpu.VMEM((heads, rows, rows), BF16),
+                pltpu.VMEM((heads, rows, rows), BF16), pltpu.VMEM((heads, rows, rows), BF16),
+                pltpu.VMEM((rows, HD), F32), pltpu.VMEM((rows, HD), F32),
+                pltpu.VMEM((heads, rows, HD), F32), pltpu.VMEM((heads, rows, HD), F32),
                 page, page, page, page, page,
                 pltpu.VMEM((n_tp, 8, rows), F32),
                 pltpu.VMEM((n_seq, heads, HD), F32),
                 pltpu.VMEM((n_dp, heads, HD), F32),
                 pltpu.VMEM((heads, HD), F32),
                 sems((5,)), sems((4 * heads + 1,)),
-                sems((heads,)), sems((heads,)), sems((heads,)), sems((heads,)),
+                sems((chunks,)), sems((chunks,)), sems((chunks,)), sems((chunks,)),
                 sems((max(n_tp - 1, 1),)), sems((max(n_tp - 1, 1),)),
                 sems((max(n_seq - 1, 1),)), sems((max(n_seq - 1, 1),)),
                 sems((max(n_dp - 1, 1),)), sems((max(n_dp - 1, 1),)),
             ],
-            compiler_params=pltpu.CompilerParams(collective_id=0, has_side_effects=True),
-        )(flat(queries), flat(keys), flat(values), out_gain.reshape(heads, HD), flat(grad_out))
+            compiler_params=pltpu.CompilerParams(collective_id=0, has_side_effects=True, vmem_limit_bytes=32 << 20
+            ),
+        )(
+            *(
+                pltpu.with_memory_space_constraint(x, pltpu.HBM)
+                for x in (
+                    flat(queries), flat(keys), flat(values),
+                    out_gain.reshape(heads, HD), flat(grad_out),
+                )
+            )
+        )
+        outs = pl.pallas_call(
+            write_out,
+            out_shape=tuple(jax.ShapeDtypeStruct(x.shape, x.dtype) for x in outs),
+            in_specs=[pl.BlockSpec(memory_space=pl.ANY)] * 5,
+            out_specs=[pl.BlockSpec(memory_space=pl.ANY)] * 5,
+            scratch_shapes=[sems((5,))],
+            compiler_params=pltpu.CompilerParams(vmem_limit_bytes=8 << 20),
+        )(*outs)
         return tuple(x.reshape(shape) for x in outs[:4]) + (outs[4].reshape(width),)
 
     spec = P("dp", "seq", "tp")

time: 56.8 us -> 51.1 us (0.90)
  local copies, waits for them, and re-layouts: 5.1 us -> 0 us
    unnamed x13 -> x0, local copies, waits for them, and re-layouts: 5.1 us -> none
    pallas_call x1, Pallas kernels: 50.8 us -> 49.3 us  [local(): pl.pallas_call(functools.partial(kernel, n_seq, n_tp, n_dp), out_shape=(m...]
    pallas_call x0 -> x1, Pallas kernels: none -> 1.01 us  [local(): pl.pallas_call(write_out, out_shape=tuple((jax.ShapeDtypeStruct(x.shape,...]
where the time goes in v2:
time: 51.1 us; the launch traced here: 51 us
  Pallas kernels  50.3 us (98%)
  between operations  0.64 us (1%)
    pallas_call x1, Pallas kernels, local(): pl.pallas_call(functools.partial(kernel, n_seq, n_tp, n_dp), out_shape=(m...  49.3 us

profile of v2, /device:TPU:0, one launch (start us, length us, event | category | flops | bytes accessed | tf_op | source)
XLA Modules:
  0.0 51.0 jit_solution(3387233285637563120)
XLA Ops:
  0.6 49.3 %shard_map.92 = (bf16[128,1024]{1,0:T(8,128)(2,1)S(1)}, bf16[128,1024]{1,0:T(8,128)(2,1)S(1)}, bf16[128,1024]{1,0:T(8,128)(2,1)S(1)}, bf16[128,1024]{1,0:T(8,128)(2,1)S(1)}, f32[8,128]{1,0:T(8,128)S(1)}) custom-call(bf16[128,1024]{1,0:T(8,128)(2,1)} %bitcast.10, bf16[128,1024]{1,0:T(8,128)(2,1)} %bitcast.11, bf16[128,1024]{1,0:T(8,128)(2,1)} %bitcast.12, ...), custom_call_target="tpu_custom_call" | custom-call | tf_op jit(solution)/shard_map/pallas_call | solution.py:330
  50.0 1.0 %shard_map.93 = (bf16[128,1024]{1,0:T(8,128)(2,1)}, bf16[128,1024]{1,0:T(8,128)(2,1)}, bf16[128,1024]{1,0:T(8,128)(2,1)}, bf16[128,1024]{1,0:T(8,128)(2,1)}, f32[8,128]{1,0:T(8,128)}) custom-call(bf16[128,1024]{1,0:T(8,128)(2,1)S(1)} %get-tuple-element.15.refs_0_, bf16[128,1024]{1,0:T(8,128)(2,1)S(1)} %get-tuple-element.16.refs_1_, ...), custom_call_target="tpu_custom_call" | custom-call | tf_op jit(solution)/shard_map/pallas_call | solution.py:364

commit v3 on v2

--- a/solution.py
+++ b/solution.py
@@ -38,10 +38,11 @@
     q_ref, k_ref, v_ref, gain_ref, g_ref,
     prior, total, later, total_back,
     att, scores, mixed, squares, crossed, dk_part, dv_part, up, normed, dq, dk, dv,
-    stat, gain_seq, gain_dp, gg,
+    stat, gain_seq, gain_dp, gg, gain_back,
     in_sem, out_sem,
     up_send, up_recv, down_send, down_recv,
     stat_send, stat_recv, gs_send, gs_recv, gd_send, gd_recv,
+    gb_send, gb_recv,
 ):
     rows, width = q_ref.shape
     heads = width // HD
@@ -58,9 +59,11 @@
     def peers(axis, me, size):
         return [{axis: lax.rem(me + i, size)} for i in range(1, size)]
 
-    everyone = peers("seq", z, n_seq) + peers("tp", t, n_tp) + peers("dp", d, n_dp)
+    greeted = peers("tp", t, n_tp) + peers("dp", d, n_dp)
+    if n_seq > 1:
+        greeted.append({"seq": below})
     barrier = pltpu.get_barrier_semaphore()
-    for peer in everyone:
+    for peer in greeted:
         pl.semaphore_signal(barrier, inc=1, device_id=peer, device_id_type=MESH)
 
     loads = [
@@ -114,7 +117,7 @@
     for h in range(heads):
         total[h] = dot(k_ref[:, head(h)], v_ref[:, head(h)], 0, 0)
         if h == 0:
-            pl.semaphore_wait(barrier, len(everyone))
+            pl.semaphore_wait(barrier, len(greeted))
         if n_seq > 1:
             @pl.when(first)
             def _():
@@ -208,9 +211,25 @@
     back_state(0)
     for h in range(1, heads):
         upstream(h)
-    seq_moves = all_send(gain_seq, "seq", z, n_seq, gs_send, gs_recv)
-    for move in seq_moves:
-        move.start()
+
+    def gain_to_first(source):
+        return pltpu.make_async_remote_copy(
+            src_ref=gain_seq.at[source], dst_ref=gain_seq.at[source],
+            send_sem=gs_send.at[source], recv_sem=gs_recv.at[source],
+            device_id={"seq": 0}, device_id_type=MESH,
+        )
+
+    def gain_from_first(target):
+        return pltpu.make_async_remote_copy(
+            src_ref=gg, dst_ref=gain_back,
+            send_sem=gb_send.at[target], recv_sem=gb_recv.at[target],
+            device_id={"seq": target}, device_id_type=MESH,
+        )
+
+    @pl.when(jnp.logical_not(first))
+    def _():
+        gain_to_first(z).start()
+
     for h in range(1, heads):
         back_state(h)
 
@@ -251,14 +270,28 @@
         store(dv.at[:, head(h)], dv_out.at[:, head(h)])
 
     def gain_middle():
-        for move in seq_moves:
-            move.wait_recv()
-        gain_sum = gain_seq[0]
-        for i in range(1, n_seq):
-            gain_sum = gain_sum + gain_seq[i]
-        gain_dp[d] = gain_sum
-        for move in dp_moves:
-            move.start()
+        @pl.when(first)
+        def _():
+            for source in range(1, n_seq):
+                gain_to_first(source).wait_recv()
+            gain_sum = gain_seq[0]
+            for i in range(1, n_seq):
+                gain_sum = gain_sum + gain_seq[i]
+            gain_dp[d] = gain_sum
+            for move in dp_moves:
+                move.start()
+
+    def gain_end():
+        @pl.when(first)
+        def _():
+            for move in dp_moves:
+                move.wait_recv()
+            gain_sum = gain_dp[0]
+            for i in range(1, n_dp):
+                gain_sum = gain_sum + gain_dp[i]
+            gg[...] = gain_sum
+            for target in range(1, n_seq):
+                gain_from_first(target).start()
 
     block_work = [
         functools.partial(work, h)
@@ -275,20 +308,31 @@
             slots[h * PIECES + 1].append(functools.partial(dv_of, h - 1))
         slots[h * PIECES + 2].append(block_work[half + 2 * h])
         slots[h * PIECES + 3].append(block_work[half + 2 * h + 1])
-    slots[(3 * heads // 4) * PIECES].append(gain_middle)
+    slots[0].append(gain_middle)
+    slots[heads // 4 * PIECES].append(gain_end)
     relay_all(total_back, later, move_down, last, first, slots)
     dk_of(heads - 1)
     dv_of(heads - 1)
 
-    for move in dp_moves:
-        move.wait_recv()
-    gain_sum = gain_dp[0]
-    for i in range(1, n_dp):
-        gain_sum = gain_sum + gain_dp[i]
-    gg[...] = gain_sum
-    store(gg, gg_out)
-
-    for move in stat_moves + seq_moves + dp_moves:
+    gg_copy = pltpu.make_async_copy(gg, gg_out, out_sem.at[4 * heads])
+
+    @pl.when(first)
+    def _():
+        gg_copy.start()
+        for move in dp_moves:
+            move.wait_send()
+        for target in range(1, n_seq):
+            gain_from_first(target).wait_send()
+
+    back_copy = pltpu.make_async_copy(gain_back, gg_out, out_sem.at[4 * heads])
+
+    @pl.when(jnp.logical_not(first))
+    def _():
+        gain_from_first(z).wait_recv()
+        back_copy.start()
+        gain_to_first(z).wait_send()
+
+    for move in stat_moves:
         move.wait_send()
     if n_seq > 1:
         @pl.when(jnp.logical_not(last))
@@ -304,6 +348,14 @@
                     move_down(h, p).wait_send()
     for copy in stores:
         copy.wait()
+
+    @pl.when(first)
+    def _():
+        gg_copy.wait()
+
+    @pl.when(jnp.logical_not(first))
+    def _():
+        back_copy.wait()
 
 
 def write_out(*refs):
@@ -343,12 +395,13 @@
                 pltpu.VMEM((n_tp, 8, rows), F32),
                 pltpu.VMEM((n_seq, heads, HD), F32),
                 pltpu.VMEM((n_dp, heads, HD), F32),
-                pltpu.VMEM((heads, HD), F32),
+                pltpu.VMEM((heads, HD), F32), pltpu.VMEM((heads, HD), F32),
                 sems((5,)), sems((4 * heads + 1,)),
                 sems((chunks,)), sems((chunks,)), sems((chunks,)), sems((chunks,)),
                 sems((max(n_tp - 1, 1),)), sems((max(n_tp - 1, 1),)),
-                sems((max(n_seq - 1, 1),)), sems((max(n_seq - 1, 1),)),
+                sems((n_seq,)), sems((n_seq,)),
                 sems((max(n_dp - 1, 1),)), sems((max(n_dp - 1, 1),)),
+                sems((n_seq,)), sems((n_seq,)),
             ],
             compiler_params=pltpu.CompilerParams(collective_id=0, has_side_effects=True, vmem_limit_bytes=32 << 20
             ),

time: 51.1 us -> 47.7 us (0.933)
  Pallas kernels: 50.3 us -> 46.9 us
    pallas_call x1, Pallas kernels: 49.3 us -> 45.9 us  [local(): pl.pallas_call(functools.partial(kernel, n_seq, n_tp, n_dp), out_shape=(m...]
where the time goes in v3:
time: 47.7 us; the launch traced here: 47.6 us
  Pallas kernels  46.9 us (98%)
  between operations  0.64 us (1%)
    pallas_call x1, Pallas kernels, local(): pl.pallas_call(functools.partial(kernel, n_seq, n_tp, n_dp), out_shape=(m...  45.9 us
    pallas_call x1, Pallas kernels, local(): pl.pallas_call(write_out, out_shape=tuple((jax.ShapeDtypeStruct(x.shape,...  1.01 us

profile of v3, /device:TPU:0, one launch (start us, length us, event | category | flops | bytes accessed | tf_op | source)
XLA Modules:
  0.0 47.6 jit_solution(9446716084585982821)
XLA Ops:
  0.6 45.9 %shard_map.92 = (bf16[128,1024]{1,0:T(8,128)(2,1)S(1)}, bf16[128,1024]{1,0:T(8,128)(2,1)S(1)}, bf16[128,1024]{1,0:T(8,128)(2,1)S(1)}, bf16[128,1024]{1,0:T(8,128)(2,1)S(1)}, f32[8,128]{1,0:T(8,128)S(1)}) custom-call(bf16[128,1024]{1,0:T(8,128)(2,1)} %bitcast.10, bf16[128,1024]{1,0:T(8,128)(2,1)} %bitcast.11, bf16[128,1024]{1,0:T(8,128)(2,1)} %bitcast.12, ...), custom_call_target="tpu_custom_call" | custom-call | tf_op jit(solution)/shard_map/pallas_call | solution.py:382
  46.5 1.0 %shard_map.93 = (bf16[128,1024]{1,0:T(8,128)(2,1)}, bf16[128,1024]{1,0:T(8,128)(2,1)}, bf16[128,1024]{1,0:T(8,128)(2,1)}, bf16[128,1024]{1,0:T(8,128)(2,1)}, f32[8,128]{1,0:T(8,128)}) custom-call(bf16[128,1024]{1,0:T(8,128)(2,1)S(1)} %get-tuple-element.15.refs_0_, bf16[128,1024]{1,0:T(8,128)(2,1)S(1)} %get-tuple-element.16.refs_1_, ...), custom_call_target="tpu_custom_call" | custom-call | tf_op jit(solution)/shard_map/pallas_call | solution.py:417
